TPU v7x, 32 devices: a whole 2x2x4 slice. The times are simulated.
32 devices in a mesh: dp: 2 (over x), expert: 16 (over z, y, core).
Axes of the slice: x: 2, y: 2, z: 4, core: 2. Of those that a mesh axis runs over, the one named last changes fastest.
Arguments:
- query_nope: bfloat16 [16, 128, 2048], P('expert', None, 'dp'), may hold values from -6 to 6
- query_rope: bfloat16 [16, 128, 1024], P('expert', None, 'dp'), may hold values from -8 to 8
- latent_new: bfloat16 [16, 128, 512], P('expert'), may hold values from -6 to 6
- key_rope: bfloat16 [16, 128, 64], P('expert'), may hold values from -8 to 8
- latent_pages: bfloat16 [16, 8, 64, 512], P('expert', 'dp'), may hold values from -6 to 6
- rope_pages: bfloat16 [16, 8, 4096], P('expert', 'dp'), may hold values from -6 to 6
- page_table: int32 [16, 8], P('expert'), may hold values from 0 to 7, each once within a row
- prefix_lengths: int32 [16], P('expert'), may hold values from 0 to 512, as said below
- residual: bfloat16 [16, 128, 2048], P('expert'), may hold values from -60 to 60
- key_up: bfloat16 [16, 128, 512], P('dp'), may hold values from -0.5 to 0.5
- value_up: bfloat16 [16, 512, 128], P('dp'), may hold values from -0.25 to 0.25
- out_weight: bfloat16 [2048, 2048], P('dp'), may hold values from -0.125 to 0.125
- norm_gain: float32 [2048], replicated, may hold values from 0.1 to 1.9
- expert_in: bfloat16 [16, 1408, 2, 2048], P('expert', 'dp'), may hold values from -0.125 to 0.125
- expert_down: bfloat16 [16, 1408, 2048], P('expert', 'dp'), may hold values from -0.15625 to 0.15625
- expert_ids: int32 [16, 128, 6], P('expert'), may hold values from 0 to 15, all different within a row; in each aligned block of 64 rows (0 to 63, 64 to 127, ..., all dimensions but the last counted through in order) at most 48 rows name the same one
- expert_weights: float32 [16, 128, 6], P('expert'), may hold values from 0.05 to 0.4
Outputs:
- layer_out: bfloat16 [16, 128, 2048], P('expert', 'dp')
- expert_mix: bfloat16 [16, 128, 2048], P('expert', 'dp')
Inputs may be any that keep to these rules, and one draw needn't show every extreme that they name: `prefix_lengths`: some request's prefix fills all of its 8 page slots. `page_table`: each row names every page slot of its request once; entry j holds positions j * 64 to (j + 1) * 64 - 1. `expert_ids`: each row names 6 distinct experts; in each aligned block of 64 rows of a request (blocks along the first two dimensions taken together) no expert is named more than 48 times, and that many is reached.
All inputs are finite; a program needn't handle non-finite values.
Results may differ from a plain program's by a relative error of at most 0.019.
Values may be sent and summed in bfloat16 or wider, within the bound.
A program may use at most 128 MiB of HBM per device.

v0:
```python
import jax
import jax.numpy as jnp
from jax import lax
from jax.sharding import PartitionSpec as P

HD = 128
RD = 64
LAT = 512
TOP = 6
PAGE = 64


EPS = 1e-06
NEG = -1e30


def norm_rows(hidden, norm_gain):
    power = jnp.mean(hidden * hidden, axis=-1, keepdims=True)
    return (hidden * lax.rsqrt(power + EPS) * norm_gain).astype(jnp.bfloat16)


def expert_apply(tokens, expert_in, expert_down):
    flat = tokens.reshape(-1, tokens.shape[-1])
    dims = (((1,), (1,)), ((), ()))
    gate_act = lax.dot_general(
        flat, expert_in[0, :, 0, :], dims, preferred_element_type=jnp.float32
    )
    up_act = lax.dot_general(flat, expert_in[0, :, 1, :], dims, preferred_element_type=jnp.float32)
    units = (jax.nn.silu(gate_act) * up_act).astype(jnp.bfloat16)
    part = jnp.dot(units, expert_down[0], preferred_element_type=jnp.float32).astype(jnp.bfloat16)
    return part.reshape(tokens.shape)


def slot_table(ids, block_rows, experts, stride):
    blocks = ids.reshape(-1, block_rows * TOP)
    onehot = (blocks[..., None] == jnp.arange(experts)[None, None, :]).astype(jnp.int32)
    before = jnp.cumsum(onehot, axis=1) - onehot
    rank = jnp.sum(before * onehot, axis=-1)
    return (blocks * stride + rank).reshape(-1)


def pack_rows(tokens, slots, total):
    source = jnp.arange(slots.shape[0]) // TOP
    row_of = jnp.zeros((total,), jnp.int32).at[slots].set(source)
    filled = jnp.zeros((total,), jnp.bool_).at[slots].set(True)
    return jnp.where(filled[:, None], tokens[row_of], jnp.zeros((), tokens.dtype))


def combine(returned, slots, weights):
    values = returned.reshape(-1, returned.shape[-1])[slots]
    values = values.reshape(weights.shape[0], weights.shape[1], -1)
    return jnp.einsum("tk,tkd->td", weights, values)


def per_device(
    query_nope,
    query_rope,
    latent_new,
    key_rope,
    latent_pages,
    rope_pages,
    page_table,
    prefix_lengths,
    residual,
    key_up,
    value_up,
    out_weight,
    norm_gain,
    expert_in,
    expert_down,
    expert_ids,
    expert_weights,
):
    groups = lax.axis_size("dp")
    experts_all = lax.axis_size("expert") * expert_in.shape[0]
    tokens_col = query_nope.shape[1]
    block_rows = tokens_col // groups
    cap_block = min(block_rows, max(2, 2 * block_rows * TOP // experts_all))
    heads_here = key_up.shape[0]
    pages_lat, pages_rope = (
        lax.all_gather(latent_pages[0], "dp", axis=0, tiled=True),
        lax.all_gather(rope_pages[0], "dp", axis=0, tiled=True),
    )
    page_count = pages_lat.shape[0]
    table = page_table[0]
    inverse = jnp.sum(
        jnp.where(
            table[:, None] == jnp.arange(page_count)[None, :], jnp.arange(page_count)[:, None], 0
        ),
        axis=0,
    )
    positions = (inverse[:, None] * PAGE + jnp.arange(PAGE)[None, :]).reshape(-1)
    prefix_ok = positions < prefix_lengths[0]
    keys_lat = jnp.concatenate([pages_lat.reshape(-1, LAT), latent_new[0]], axis=0)
    keys_rope = jnp.concatenate([pages_rope.reshape(-1, RD), key_rope[0]], axis=0)
    heads_nope = query_nope[0].reshape(tokens_col, heads_here, HD)
    query_lat = jnp.einsum(
        "thd,hdc->thc", heads_nope, key_up, preferred_element_type=jnp.float32
    ).astype(jnp.bfloat16)
    heads_rope = query_rope[0].reshape(tokens_col, heads_here, RD)
    scale = 1.0 / (HD + RD) ** 0.5
    scores = (
        jnp.einsum("thc,kc->thk", query_lat, keys_lat, preferred_element_type=jnp.float32)
        + jnp.einsum("thr,kr->thk", heads_rope, keys_rope, preferred_element_type=jnp.float32)
    ) * scale
    causal = jnp.arange(tokens_col)[None, :] <= jnp.arange(tokens_col)[:, None]
    allowed = jnp.concatenate(
        [jnp.broadcast_to(prefix_ok[None, :], (tokens_col, prefix_ok.shape[0])), causal], axis=1
    )[:, None, :]
    masked = jnp.where(allowed, scores, NEG)
    peak = jnp.max(masked, axis=-1, keepdims=True)
    expo = jnp.where(allowed, jnp.exp(masked - peak), 0.0)
    total = jnp.sum(expo, axis=-1, keepdims=True)
    probs = expo.astype(jnp.bfloat16)
    attn_latent = (
        jnp.einsum("thk,kc->thc", probs, keys_lat, preferred_element_type=jnp.float32) / total
    ).astype(jnp.bfloat16)
    heads_out = jnp.einsum(
        "thc,hcd->thd", attn_latent, value_up, preferred_element_type=jnp.float32
    ).astype(jnp.bfloat16)
    partial_out = jnp.dot(
        heads_out.reshape(tokens_col, heads_here * HD),
        out_weight,
        preferred_element_type=jnp.float32,
    )
    attended = lax.psum(partial_out.astype(jnp.bfloat16), "dp").astype(jnp.float32)
    hidden = residual[0].astype(jnp.float32) + attended
    start = lax.axis_index("dp") * block_rows
    hidden_mine = lax.dynamic_slice_in_dim(hidden, start, block_rows, 0)
    normed = norm_rows(hidden_mine, norm_gain)
    ids_mine = lax.dynamic_slice_in_dim(expert_ids[0], start, block_rows, 0)
    weights_mine = lax.dynamic_slice_in_dim(expert_weights[0], start, block_rows, 0)
    slots = slot_table(ids_mine, block_rows, experts_all, cap_block)
    outgoing = pack_rows(normed, slots, experts_all * cap_block).reshape(experts_all, cap_block, -1)
    everyone = lax.all_gather(
        lax.all_to_all(outgoing, "expert", split_axis=0, concat_axis=0, tiled=True),
        "dp",
        axis=0,
        tiled=True,
    )
    part = expert_apply(everyone, expert_in, expert_down)
    summed = lax.psum_scatter(
        part.astype(jnp.float32).astype(jnp.bfloat16), "dp", scatter_dimension=0, tiled=True
    ).astype(jnp.float32)
    returned = lax.all_to_all(
        summed.astype(jnp.bfloat16), "expert", split_axis=0, concat_axis=0, tiled=True
    ).astype(summed.dtype)
    mixture = combine(returned, slots, weights_mine)
    layer_out = (hidden_mine + mixture).astype(jnp.bfloat16)[None]
    return (layer_out, mixture.astype(jnp.bfloat16)[None])


def solution(mesh):
    return jax.shard_map(
        per_device,
        mesh=mesh,
        in_specs=(
            P("expert", None, "dp"),
            P("expert", None, "dp"),
            P("expert", None, None),
            P("expert", None, None),
            P("expert", "dp", None, None),
            P("expert", "dp", None),
            P("expert", None),
            P("expert"),
            P("expert", None, None),
            P("dp", None, None),
            P("dp", None, None),
            P("dp", None),
            P(),
            P("expert", "dp", None, None),
            P("expert", "dp", None),
            P("expert", None, None),
            P("expert", None, None),
        ),
        out_specs=(P("expert", "dp", None), P("expert", "dp", None)),
        check_vma=False,
    )
```

profile of v0, /device:TPU:13, one launch (start us, length us, event | category | flops | bytes accessed | tf_op | source)
XLA Modules:
  0.0 443.6 jit_solution(2235511054442447366)
XLA Ops:
  7.2 8.2 %all-gather = bf16[1,8,64,512]{3,2,0,1:T(8,128)(2,1)S(1)} all-gather(bf16[1,4,64,512]{3,2,0,1:T(8,128)(2,1)} %bitcast.118), channel_id=2, replica_groups=mesh['dp'=2,'expert'=16] {'dp'}, dimensions={1}, use_global_device_ids=true | all-gather | bytes 786432 | tf_op jit(solution)/shard_map/all_gather | solution.py:81
  15.4 1.7 copy.91
  17.1 0.8 copy.67
  18.0 3.8 all-gather.1
  21.7 1.0 reduce.1
  22.7 1.0 reshape.226
  24.5 1.7 copy.69
  28.4 4.1 fusion.6
  32.5 4.9 %fusion.38 = (f32[128,8]{0,1:T(8,128)}, bf16[128,8,640]{2,0,1:T(8,128)(2,1)}) fusion(pred[128,640]{1,0:T(8,128)(4,1)} %pad_add_fusion, f32[128,8,640]{2,0,1:T(8,128)} %fusion.6, bf16[128,8,64]{0,2,1:T(8,128)(2,1)} %bitcast.124, bf16[128,64]{0,1:T(8,128)(2,1)S(1)} %bitcast.129, bf16[512,64]{0,1:T(8,128)(2,1)} %copy.68), kind=kOutput, calls=%fused_computation.77 | convolution fusion | flops 88638080 | bytes 4231168 | tf_op jit(solution)/shard_map/sub | solution.py:112
  37.4 3.6 fusion.11
  41.0 3.9 convolution_convert_fusion.1
  45.3 0.9 reduce-window.6
  46.9 2.9 scatter_custom_fusion.1
  49.9 2.0 scatter_custom_fusion
  52.0 24.7 %all-reduce.2.cloned.1.call-done = bf16[128,2048]{1,0:T(8,128)(2,1)} async-done(((bf16[128,2048]{1,0:T(8,128)(2,1)}), bf16[128,2048]{1,0:T(8,128)(2,1)}) %all-reduce.2.cloned.1.call-update) | async-done | bytes 524304 | tf_op jit(solution)/shard_map/psum | solution.py:126
  76.7 1.1 multiply_reduce_fusion
  77.9 1.1 multiply_convert_fusion.1
  79.0 4.3 gather_fusion
  83.3 2.2 broadcast_select_fusion
  85.5 76.2 %all_to_all.10 = bf16[16,48,2048]{2,1,0:T(8,128)(2,1)} all-to-all(bf16[16,48,2048]{2,1,0:T(8,128)(2,1)S(1)} %broadcast_select_fusion), channel_id=1, replica_groups=mesh['dp'=2,'expert'=16] {'expert'}, dimensions={0} | all-to-all | bytes 6291456 | tf_op jit(solution)/shard_map/all_to_all | solution.py:136
  161.9 12.7 %fusion.37 = (bf16[1,704,1,2048]{3,2,1,0:T(2,128)(2,1)}, bf16[1,704,1,2048]{3,2,1,0:T(2,128)(2,1)}) fusion(bf16[1,704,2,2048]{3,2,1,0:T(2,128)(2,1)} %param.30), kind=kLoop, calls=%fused_computation.76 | loop fusion | bytes 11534336 | tf_op jit(solution)/shard_map/slice | solution.py:28
  174.6 66.2 %all-gather.4.cloned.1.call-done = bf16[32,48,2048]{2,1,0:T(8,128)(2,1)} async-done(((bf16[16,48,2048]{2,1,0:T(8,128)(2,1)}), bf16[32,48,2048]{2,1,0:T(8,128)(2,1)}) %all-gather.4.cloned.1.call-update) | async-done | bytes 6291472 | tf_op jit(solution)/shard_map/all_gather | solution.py:135
  240.8 11.6 %fusion.1 = f32[1536,704]{0,1:T(8,128)} fusion(bf16[1536,2048]{1,0:T(8,128)(2,1)} %bitcast.127, bf16[1,704,1,2048]{3,2,1,0:T(2,128)(2,1)} %get-tuple-element.5), kind=kOutput, calls=%fused_computation.10 | convolution fusion | flops 4429185024 | bytes 13500416 | tf_op jit(solution)/shard_map/dot_general | solution.py:25
  252.4 19.8 %convolution_convert_fusion = bf16[1536,2048]{1,0:T(8,128)(2,1)} fusion(bf16[1,704,2048]{2,1,0:T(8,128)(2,1)S(1)} %copy-done, f32[1536,704]{0,1:T(8,128)} %fusion.1, bf16[1536,2048]{1,0:T(8,128)(2,1)} %bitcast.128, bf16[1,704,1,2048]{3,2,1,0:T(2,128)(2,1)} %get-tuple-element.4), kind=kOutput, calls=%fused_computation.5 | convolution fusion | flops 8868003840 | bytes 22675456 | tf_op jit(solution)/shard_map/dot_general | solution.py:30
  272.3 77.3 %reduce-scatter.2.cloned.1.call-done = bf16[16,48,2048]{2,1,0:T(8,128)(2,1)} async-done(((bf16[32,48,2048]{2,1,0:T(8,128)(2,1)}), bf16[16,48,2048]{2,1,0:T(8,128)(2,1)}) %reduce-scatter.2.cloned.1.call-update) | async-done | bytes 3145744 | tf_op jit(solution)/shard_map/reduce_scatter | solution.py:142
  349.6 6.5 %all-to-all-start.1 = ((bf16[16,48,2048]{2,1,0:T(8,128)(2,1)}), bf16[16,48,2048]{2,1,0:T(8,128)(2,1)S(1)}, u32[]{:S(2)}, u32[]{:S(2)}) async-start(bf16[16,48,2048]{2,1,0:T(8,128)(2,1)} %reduce-scatter.2.cloned.1.call-done), calls=%async_computation.2 | async-start | bytes 6291456 | tf_op jit(solution)/shard_map/all_to_all | solution.py:145
  356.3 69.7 %all-to-all-done.1 = bf16[16,48,2048]{2,1,0:T(8,128)(2,1)S(1)} async-done(((bf16[16,48,2048]{2,1,0:T(8,128)(2,1)}), bf16[16,48,2048]{2,1,0:T(8,128)(2,1)S(1)}, u32[]{:S(2)}, u32[]{:S(2)}) %all-to-all-start.1) | async-done | bytes 3145760 | tf_op jit(solution)/shard_map/all_to_all | solution.py:145
  425.9 3.1 gather_fusion.1
  429.1 3.9 reshape.236
  432.9 2.3 fusion.40
  435.3 0.9 copy.111
  436.1 0.9 fusion.16
  (58 shorter events, 4.0 us)
Async XLA Ops:
  7.2 245.2 %copy-start = (bf16[1,704,2048]{2,1,0:T(8,128)(2,1)S(1)}, bf16[1,704,2048]{2,1,0:T(8,128)(2,1)}, u32[]{:S(2)}) copy-start(bf16[1,704,2048]{2,1,0:T(8,128)(2,1)} %param.31) | copy-start | bytes 8650756
  7.2 69.5 %all-reduce.2.cloned.1.call-start = ((), (), s32[]{:S(2)}) async-start(), calls=%async_computation.3 | async-start | bytes 1048576 | tf_op jit(solution)/shard_map/psum | solution.py:126
  28.4 4.1 copy-start.9
  32.5 4.9 %copy-start.5 = (bf16[1,128,512]{2,1,0:T(8,128)(2,1)S(1)}, bf16[1,128,512]{2,1,0:T(8,128)(2,1)}, u32[]{:S(2)}) copy-start(bf16[1,128,512]{2,1,0:T(8,128)(2,1)} %param.19) | copy-start | bytes 393220
  41.0 3.9 copy-start.7
  41.0 35.7 %copy-start.2 = (bf16[1,128,2048]{2,1,0:T(8,128)(2,1)S(1)}, bf16[1,128,2048]{2,1,0:T(8,128)(2,1)}, u32[]{:S(2)}) copy-start(bf16[1,128,2048]{2,1,0:T(8,128)(2,1)} %param.25) | copy-start | bytes 1572868
  41.0 36.8 %copy-start.6 = (f32[2048]{0:T(1024)S(1)}, f32[2048]{0:T(1024)}, u32[]{:S(2)}) copy-start(f32[2048]{0:T(1024)} %param.29) | copy-start | bytes 24580
  44.9 195.9 %all-gather.4.cloned.1.call-start = ((), (), s32[]{:S(2)}) async-start(), calls=%async_computation.4 | async-start | bytes 9437184 | tf_op jit(solution)/shard_map/all_gather | solution.py:135
  161.6 187.9 %reduce-scatter.2.cloned.1.call-start = ((), (), s32[]{:S(2)}) async-start(), calls=%async_computation.5 | async-start | bytes 9437184 | tf_op jit(solution)/shard_map/reduce_scatter | solution.py:142
  272.3 83.8 %copy-start.8 = (f32[1,128,6]{1,0,2:T(1,128)S(1)}, f32[1,128,6]{1,0,2:T(1,128)}, u32[]{:S(2)}) copy-start(f32[1,128,6]{1,0,2:T(1,128)} %param.33) | copy-start | bytes 9220
  349.6 76.4 %all-to-all-start.1 = ((bf16[16,48,2048]{2,1,0:T(8,128)(2,1)}), bf16[16,48,2048]{2,1,0:T(8,128)(2,1)S(1)}, u32[]{:S(2)}, u32[]{:S(2)}) async-start(bf16[16,48,2048]{2,1,0:T(8,128)(2,1)} %reduce-scatter.2.cloned.1.call-done), calls=%async_computation.2 | async-start | bytes 6291456 | tf_op jit(solution)/shard_map/all_to_all | solution.py:145
  429.0 7.1 %copy-start.3 = (bf16[1,128,2048]{2,1,0:T(8,128)(2,1)S(1)}, bf16[1,128,2048]{2,1,0:T(8,128)(2,1)}, u32[]{:S(2)}) copy-start(bf16[1,128,2048]{2,1,0:T(8,128)(2,1)} %param.25) | copy-start | bytes 1572868
  429.0 8.0 %copy-start.1 = (bf16[1,704,2048]{2,1,0:T(8,128)(2,1)S(1)}, bf16[1,704,2048]{2,1,0:T(8,128)(2,1)}, u32[]{:S(2)}) copy-start(bf16[1,704,2048]{2,1,0:T(8,128)(2,1)} %param.31) | copy-start | bytes 8650756
  432.9 3.2 copy-start.4
Sparse Core Ops, SparseCore 0:
  45.0 31.6 all-reduce.1
  161.7 78.9 all-gather.3
  272.4 77.1 reduce-scatter.1
where the time goes:
time: 444 us
  waiting for transfers between devices  238 us (54%)
  blocking collectives  88.1 us (20%)
  matrix products  50.3 us (11%)
  local copies, waits for them, and re-layouts  36.9 us (8%)
  between operations  14.6 us (3%)
  other arithmetic  8.89 us (2%)
  starting transfers between devices  6.81 us (2%)
    reduce_scatter x1, waiting for transfers between devices, per_device(): lax.psum_scatter(part.astype(jnp.float32).astype(jnp.bfloat16), 'dp', sca...  77.3 us
    all_to_all x1, blocking collectives, per_device(): lax.all_to_all(outgoing, 'expert', split_axis=0, concat_axis=0, tiled=True)  76.2 us
    all_to_all x1, waiting for transfers between devices, per_device(): lax.all_to_all(summed.astype(jnp.bfloat16), 'expert', split_axis=0, conca...  69.7 us
    all_gather x1, waiting for transfers between devices, per_device(): lax.all_gather(lax.all_to_all(outgoing, 'expert', split_axis=0, concat_ax...  66.2 us
    psum x1, waiting for transfers between devices, per_device(): lax.psum(partial_out.astype(jnp.bfloat16), 'dp').astype(jnp.float32)  24.7 us
    dot_general x1, matrix products, expert_apply(): jnp.dot(units, expert_down[0], preferred_element_type=jnp.float32)  19.8 us
    slice x1, local copies, waits for them, and re-layouts, expert_apply(): expert_in[0, :, 1, :]  12.7 us
    dot_general x1, matrix products, expert_apply(): lax.dot_general(flat, expert_in[0, :, 0, :], dims, preferred_element_type...  11.6 us
  transfers between devices with their start and end apart: 4, of which 4 were waited for; matrix products, arithmetic and copies ran while one was open for 4% of the time, Pallas kernels for 0%

commit v1 on v0

--- a/solution.py
+++ b/solution.py
@@ -19,7 +19,7 @@
     return (hidden * lax.rsqrt(power + EPS) * norm_gain).astype(jnp.bfloat16)
 
 
-def expert_apply(tokens, expert_in, expert_down):
+def expert_apply(tokens, gate, expert_in, expert_down):
     flat = tokens.reshape(-1, tokens.shape[-1])
     dims = (((1,), (1,)), ((), ()))
     gate_act = lax.dot_general(
@@ -27,29 +27,8 @@
     )
     up_act = lax.dot_general(flat, expert_in[0, :, 1, :], dims, preferred_element_type=jnp.float32)
     units = (jax.nn.silu(gate_act) * up_act).astype(jnp.bfloat16)
-    part = jnp.dot(units, expert_down[0], preferred_element_type=jnp.float32).astype(jnp.bfloat16)
-    return part.reshape(tokens.shape)
-
-
-def slot_table(ids, block_rows, experts, stride):
-    blocks = ids.reshape(-1, block_rows * TOP)
-    onehot = (blocks[..., None] == jnp.arange(experts)[None, None, :]).astype(jnp.int32)
-    before = jnp.cumsum(onehot, axis=1) - onehot
-    rank = jnp.sum(before * onehot, axis=-1)
-    return (blocks * stride + rank).reshape(-1)
-
-
-def pack_rows(tokens, slots, total):
-    source = jnp.arange(slots.shape[0]) // TOP
-    row_of = jnp.zeros((total,), jnp.int32).at[slots].set(source)
-    filled = jnp.zeros((total,), jnp.bool_).at[slots].set(True)
-    return jnp.where(filled[:, None], tokens[row_of], jnp.zeros((), tokens.dtype))
-
-
-def combine(returned, slots, weights):
-    values = returned.reshape(-1, returned.shape[-1])[slots]
-    values = values.reshape(weights.shape[0], weights.shape[1], -1)
-    return jnp.einsum("tk,tkd->td", weights, values)
+    part = jnp.dot(units, expert_down[0], preferred_element_type=jnp.float32)
+    return (part * gate).astype(jnp.bfloat16)
 
 
 def per_device(
@@ -75,7 +54,6 @@
     experts_all = lax.axis_size("expert") * expert_in.shape[0]
     tokens_col = query_nope.shape[1]
     block_rows = tokens_col // groups
-    cap_block = min(block_rows, max(2, 2 * block_rows * TOP // experts_all))
     heads_here = key_up.shape[0]
     pages_lat, pages_rope = (
         lax.all_gather(latent_pages[0], "dp", axis=0, tiled=True),
@@ -123,29 +101,32 @@
         out_weight,
         preferred_element_type=jnp.float32,
     )
-    attended = lax.psum(partial_out.astype(jnp.bfloat16), "dp").astype(jnp.float32)
-    hidden = residual[0].astype(jnp.float32) + attended
+    attended = lax.psum_scatter(
+        partial_out.astype(jnp.bfloat16), "dp", scatter_dimension=0, tiled=True
+    ).astype(jnp.float32)
     start = lax.axis_index("dp") * block_rows
-    hidden_mine = lax.dynamic_slice_in_dim(hidden, start, block_rows, 0)
+    hidden_mine = (
+        lax.dynamic_slice_in_dim(residual[0], start, block_rows, 0).astype(jnp.float32) + attended
+    )
     normed = norm_rows(hidden_mine, norm_gain)
-    ids_mine = lax.dynamic_slice_in_dim(expert_ids[0], start, block_rows, 0)
-    weights_mine = lax.dynamic_slice_in_dim(expert_weights[0], start, block_rows, 0)
-    slots = slot_table(ids_mine, block_rows, experts_all, cap_block)
-    outgoing = pack_rows(normed, slots, experts_all * cap_block).reshape(experts_all, cap_block, -1)
-    everyone = lax.all_gather(
-        lax.all_to_all(outgoing, "expert", split_axis=0, concat_axis=0, tiled=True),
-        "dp",
-        axis=0,
-        tiled=True,
+    everyone = lax.all_gather(normed, ("expert", "dp"), axis=0, tiled=True)
+    gates = jnp.sum(
+        jnp.where(
+            expert_ids[0][:, :, None] == jnp.arange(experts_all)[None, None, :],
+            expert_weights[0][:, :, None],
+            0.0,
+        ),
+        axis=1,
     )
-    part = expert_apply(everyone, expert_in, expert_down)
-    summed = lax.psum_scatter(
-        part.astype(jnp.float32).astype(jnp.bfloat16), "dp", scatter_dimension=0, tiled=True
+    all_gates = lax.all_gather(gates, "expert", axis=0, tiled=True)
+    mine = lax.axis_index("expert")
+    gate = jnp.sum(
+        jnp.where(jnp.arange(experts_all)[None, :] == mine, all_gates, 0.0), axis=1, keepdims=True
+    )
+    part = expert_apply(everyone, gate, expert_in, expert_down)
+    mixture = lax.psum_scatter(
+        part, ("expert", "dp"), scatter_dimension=0, tiled=True
     ).astype(jnp.float32)
-    returned = lax.all_to_all(
-        summed.astype(jnp.bfloat16), "expert", split_axis=0, concat_axis=0, tiled=True
-    ).astype(summed.dtype)
-    mixture = combine(returned, slots, weights_mine)
     layer_out = (hidden_mine + mixture).astype(jnp.bfloat16)[None]
     return (layer_out, mixture.astype(jnp.bfloat16)[None])
 

time: 444 us -> 368 us (0.83)
  blocking collectives: 88.1 us -> 27 us
  local copies, waits for them, and re-layouts: 36.9 us -> 18 us
  waiting for transfers between devices: 238 us -> 248 us
  starting transfers between devices: 6.81 us -> 0.12 us
    reduce_scatter x1 -> x2, waiting for transfers between devices: 77.3 us -> 199 us  [the longest x1 181 us: per_device(): lax.psum_scatter(part, ('expert', 'dp'), scatter_dimension=0, tiled=True)]
    all_to_all x1 -> x0, blocking collectives: 76.2 us -> none  [per_device(): lax.all_to_all(outgoing, 'expert', split_axis=0, concat_axis=0, tiled=True)]
    all_to_all x1 -> x0, waiting for transfers between devices: 69.7 us -> none  [per_device(): lax.all_to_all(summed.astype(jnp.bfloat16), 'expert', split_axis=0, conca...]
    psum x1 -> x0, waiting for transfers between devices: 24.7 us -> none  [per_device(): lax.psum(partial_out.astype(jnp.bfloat16), 'dp').astype(jnp.float32)]
    all_gather x1, waiting for transfers between devices: 66.2 us -> 49 us  [per_device(): everyone = lax.all_gather(normed, ('expert', 'dp'), axis=0, tiled=True)]
    all_gather x0 -> x1, blocking collectives: none -> 16.3 us  [per_device(): all_gates = lax.all_gather(gates, 'expert', axis=0, tiled=True)]
    gather x2 -> x0, local copies, waits for them, and re-layouts: 7.37 us -> none  [the longest x1 4.27 us: pack_rows(): tokens[row_of]]
    all_to_all x1 -> x0, starting transfers between devices: 6.51 us -> none  [per_device(): lax.all_to_all(summed.astype(jnp.bfloat16), 'expert', split_axis=0, conca...]
  transfers between devices with their start and end apart: 4 -> 3, of which waited for: 4 -> 3; matrix products, arithmetic and copies ran while one was open for 4% -> 4% of each run, Pallas kernels for 0% -> 0%
where the time goes in v1:
time: 368 us; the launch traced here: 366 us
  waiting for transfers between devices  248 us (67%)
  matrix products  51.3 us (14%)
  blocking collectives  27 us (7%)
  local copies, waits for them, and re-layouts  18 us (5%)
  between operations  14.7 us (4%)
  other arithmetic  6.73 us (2%)
    reduce_scatter x1, waiting for transfers between devices, per_device(): lax.psum_scatter(part, ('expert', 'dp'), scatter_dimension=0, tiled=True)  181 us
    all_gather x1, waiting for transfers between devices, per_device(): everyone = lax.all_gather(normed, ('expert', 'dp'), axis=0, tiled=True)  49 us
    dot_general x1, matrix products, expert_apply(): part = jnp.dot(units, expert_down[0], preferred_element_type=jnp.float32)  21 us
    reduce_scatter x1, waiting for transfers between devices, per_device(): lax.psum_scatter(partial_out.astype(jnp.bfloat16), 'dp', scatter_dimensio...  17.7 us
    all_gather x1, blocking collectives, per_device(): all_gates = lax.all_gather(gates, 'expert', axis=0, tiled=True)  16.3 us
    dot_general x1, matrix products, expert_apply(): lax.dot_general(flat, expert_in[0, :, 0, :], dims, preferred_element_type...  13.8 us
    slice x1, local copies, waits for them, and re-layouts, expert_apply(): expert_in[0, :, 1, :]  12.8 us
  transfers between devices with their start and end apart: 3, of which 3 were waited for; matrix products, arithmetic and copies ran while one was open for 4% of the time, Pallas kernels for 0%

profile of v1, /device:TPU:13, one launch (start us, length us, event | category | flops | bytes accessed | tf_op | source)
XLA Modules:
  0.0 365.9 jit_solution(873405155711153684)
XLA Ops:
  7.2 0.0 reduce-scatter.3.cloned.1.call-start
  8.0 0.7 select_reduce_fusion.2
  8.8 0.1 add_compare_fusion
  8.9 0.1 reshape.68
  9.0 0.8 copy.49
  9.8 3.8 %all-gather.1 = bf16[1,8,4096]{2,0,1:T(2,128)(2,1)S(1)} all-gather(bf16[1,4,4096]{2,0,1:T(2,128)(2,1)S(1)} %copy.49), channel_id=3, replica_groups=mesh['dp'=2,'expert'=16] {'dp'}, dimensions={1}, use_global_device_ids=true | all-gather | bytes 98304 | tf_op jit(solution)/shard_map/all_gather | solution.py:60
  13.6 0.4 reduce
  13.9 0.2 reshape.58
  14.1 0.7 copy.50
  14.8 1.7 copy.51
  16.5 1.7 copy.64
  18.2 6.9 %all-gather = bf16[1,8,64,512]{3,2,0,1:T(8,128)(2,1)S(1)} all-gather(bf16[1,4,64,512]{3,2,0,1:T(8,128)(2,1)} %bitcast.71), channel_id=2, replica_groups=mesh['dp'=2,'expert'=16] {'dp'}, dimensions={1}, use_global_device_ids=true | all-gather | bytes 786432 | tf_op jit(solution)/shard_map/all_gather | solution.py:59
  25.1 0.7 pad_add_fusion
  25.8 4.1 %fusion.7 = f32[128,8,640]{2,0,1:T(8,128)} fusion(bf16[8,128,512]{2,1,0:T(8,128)(2,1)} %param.26, bf16[128,512]{1,0:T(8,128)(2,1)} %bitcast.75, bf16[512,512]{1,0:T(8,128)(2,1)S(1)} %bitcast.68, bf16[128,8,128]{2,1,0:T(8,128)(2,1)} %bitcast.70), kind=kOutput, calls=%fused_computation.16 | convolution fusion | flops 807141376 | bytes 4587520 | tf_op jit(solution)/shard_map/thc,kc->thk/dot_general | solution.py:81
  29.9 4.9 %fusion.27 = (f32[128,8]{0,1:T(8,128)}, bf16[128,8,640]{2,0,1:T(8,128)(2,1)}) fusion(pred[128,640]{1,0:T(8,128)(4,1)} %pad_add_fusion, f32[128,8,640]{2,0,1:T(8,128)} %fusion.7, bf16[128,8,64]{0,2,1:T(8,128)(2,1)} %bitcast.77, bf16[128,64]{0,1:T(8,128)(2,1)S(1)} %bitcast.80, bf16[512,64]{0,1:T(8,128)(2,1)} %copy.50), kind=kOutput, calls=%fused_computation.49 | convolution fusion | flops 88638080 | bytes 4231168 | tf_op jit(solution)/shard_map/sub | solution.py:90
  34.8 3.6 fusion.12
  38.4 3.9 %convolution_convert_fusion = bf16[128,2048]{1,0:T(8,128)(2,1)} fusion(bf16[128,1024]{0,1:T(8,128)(2,1)} %bitcast.72, bf16[1024,2048]{1,0:T(8,128)(2,1)} %param.28), kind=kOutput, calls=%fused_computation.12 | convolution fusion | flops 537133056 | bytes 4980736 | tf_op jit(solution)/shard_map/dot_general | solution.py:99
  42.3 0.0 reduce-scatter.3.cloned.1.call-update
  42.3 0.0 all-gather.4.cloned.1.call-start
  42.4 17.7 %reduce-scatter.3.cloned.1.call-done = bf16[64,2048]{1,0:T(8,128)(2,1)} async-done(((bf16[128,2048]{1,0:T(8,128)(2,1)}), bf16[64,2048]{1,0:T(8,128)(2,1)}) %reduce-scatter.3.cloned.1.call-update) | async-done | bytes 262160 | tf_op jit(solution)/shard_map/reduce_scatter | solution.py:104
  60.1 1.1 multiply_reduce_fusion
  61.2 1.8 multiply_convert_fusion.2
  63.0 0.0 all-gather.4.cloned.1.call-update
  63.0 0.0 reduce-scatter.5.cloned.1.call-start
  63.1 16.3 %all_gather.15 = f32[2048,16]{0,1:T(8,128)S(1)} all-gather(f32[128,16]{0,1:T(8,128)S(1)} %select_reduce_fusion.1), channel_id=1, replica_groups=mesh['dp'=2,'expert'=16] {'expert'}, dimensions={0}, use_global_device_ids=true | all-gather | bytes 139264 | tf_op jit(solution)/shard_map/all_gather | solution.py:121
  79.4 0.1 select_reduce_fusion
  79.5 12.8 %fusion.26 = (bf16[1,704,1,2048]{3,2,1,0:T(2,128)(2,1)}, bf16[1,704,1,2048]{3,2,1,0:T(2,128)(2,1)}) fusion(bf16[1,704,2,2048]{3,2,1,0:T(2,128)(2,1)} %param.30), kind=kLoop, calls=%fused_computation.48 | loop fusion | bytes 11534336 | tf_op jit(solution)/shard_map/slice | solution.py:28
  92.3 49.0 %all-gather.4.cloned.1.call-done = bf16[2048,2048]{1,0:T(8,128)(2,1)} async-done(((bf16[64,2048]{1,0:T(8,128)(2,1)}), bf16[2048,2048]{1,0:T(8,128)(2,1)}) %all-gather.4.cloned.1.call-update) | async-done | bytes 8388624 | tf_op jit(solution)/shard_map/all_gather | solution.py:112
  141.4 13.8 %fusion.1 = f32[2048,704]{0,1:T(8,128)} fusion(bf16[2048,2048]{1,0:T(8,128)(2,1)} %all-gather.4.cloned.1.call-done, bf16[1,704,1,2048]{3,2,1,0:T(2,128)(2,1)} %get-tuple-element.3), kind=kOutput, calls=%fused_computation.5 | convolution fusion | flops 5905580032 | bytes 17039360 | tf_op jit(solution)/shard_map/dot_general | solution.py:25
  155.2 21.0 %multiply_convert_fusion = bf16[2048,2048]{1,0:T(8,128)(2,1)} fusion(f32[2048]{0:T(1024)S(1)} %select_reduce_fusion, f32[2048,704]{0,1:T(8,128)} %fusion.1, bf16[2048,2048]{1,0:T(8,128)(2,1)} %all-gather.4.cloned.1.call-done, bf16[1,704,1,2048]{3,2,1,0:T(2,128)(2,1)} %get-tuple-element.2, bf16[1,704,2048]{2,1,0:T(8,128)(2,1)S(1)} %copy-done), kind=kOutput, calls=%fused_computation.1 | convolution fusion | flops 11828199424 | bytes 28319744 | tf_op jit(solution)/shard_map/dot_general | solution.py:30
  176.2 181.3 %reduce-scatter.5.cloned.1.call-done = bf16[64,2048]{1,0:T(8,128)(2,1)} async-done(((bf16[2048,2048]{1,0:T(8,128)(2,1)}), bf16[64,2048]{1,0:T(8,128)(2,1)}) %reduce-scatter.5.cloned.1.call-update) | async-done | bytes 262160 | tf_op jit(solution)/shard_map/reduce_scatter | solution.py:127
  357.5 1.8 fusion.16
  (25 shorter events, 0.1 us)
Async XLA Ops:
  7.2 148.0 %copy-start = (bf16[1,704,2048]{2,1,0:T(8,128)(2,1)S(1)}, bf16[1,704,2048]{2,1,0:T(8,128)(2,1)}, u32[]{:S(2)}) copy-start(bf16[1,704,2048]{2,1,0:T(8,128)(2,1)} %param.31) | copy-start | bytes 8650756
  7.2 52.9 %reduce-scatter.3.cloned.1.call-start = ((), (), s32[]{:S(2)}) async-start(), calls=%async_computation.2 | async-start | bytes 786432 | tf_op jit(solution)/shard_map/reduce_scatter | solution.py:104
  16.5 13.4 %copy-start.7 = (bf16[1,128,64]{1,2,0:T(8,128)(2,1)S(1)}, bf16[1,128,64]{1,2,0:T(8,128)(2,1)}, u32[]{:S(2)}) copy-start(bf16[1,128,64]{1,2,0:T(8,128)(2,1)} %param.20) | copy-start | bytes 49156
  29.9 4.9 %copy-start.3 = (bf16[1,128,512]{2,1,0:T(8,128)(2,1)S(1)}, bf16[1,128,512]{2,1,0:T(8,128)(2,1)}, u32[]{:S(2)}) copy-start(bf16[1,128,512]{2,1,0:T(8,128)(2,1)} %param.19) | copy-start | bytes 393220
  38.4 21.6 %copy-start.2 = (bf16[1,128,2048]{2,1,0:T(8,128)(2,1)S(1)}, bf16[1,128,2048]{2,1,0:T(8,128)(2,1)}, u32[]{:S(2)}) copy-start(bf16[1,128,2048]{2,1,0:T(8,128)(2,1)} %param.25) | copy-start | bytes 1572868
  38.4 22.8 %copy-start.4 = (f32[2048]{0:T(1024)S(1)}, f32[2048]{0:T(1024)}, u32[]{:S(2)}) copy-start(f32[2048]{0:T(1024)} %param.29) | copy-start | bytes 24580
  38.4 24.6 %copy-start.5 = (s32[1,128,6]{1,0,2:T(1,128)S(1)}, s32[1,128,6]{1,0,2:T(1,128)}, u32[]{:S(2)}) copy-start(s32[1,128,6]{1,0,2:T(1,128)} %param.32) | copy-start | bytes 9220
  38.4 24.7 %copy-start.6 = (f32[1,128,6]{1,0,2:T(1,128)S(1)}, f32[1,128,6]{1,0,2:T(1,128)}, u32[]{:S(2)}) copy-start(f32[1,128,6]{1,0,2:T(1,128)} %param.33) | copy-start | bytes 9220
  42.3 99.1 %all-gather.4.cloned.1.call-start = ((), (), s32[]{:S(2)}) async-start(), calls=%async_computation.3 | async-start | bytes 8650752 | tf_op jit(solution)/shard_map/all_gather | solution.py:112
  63.0 294.5 %reduce-scatter.5.cloned.1.call-start = ((), (), s32[]{:S(2)}) async-start(), calls=%async_computation.4 | async-start | bytes 8650752 | tf_op jit(solution)/shard_map/reduce_scatter | solution.py:127
  176.2 181.4 %copy-start.1 = (bf16[64,2048]{1,0:T(8,128)(2,1)S(1)}, bf16[64,2048]{1,0:T(8,128)(2,1)}, u32[]{:S(2)}) copy-start(bf16[64,2048]{1,0:T(8,128)(2,1)} %reduce-scatter.3.cloned.1.call-done) | copy-start | bytes 786436
Sparse Core Ops, SparseCore 0:
  42.4 17.5 reduce-scatter.2
  63.6 77.7 all-gather.3
  176.3 181.1 reduce-scatter.4

commit v2 on v1

--- a/solution.py
+++ b/solution.py
@@ -1,6 +1,8 @@
 import jax
 import jax.numpy as jnp
 from jax import lax
+from jax.experimental import pallas as pl
+from jax.experimental.pallas import tpu as pltpu
 from jax.sharding import PartitionSpec as P
 
 HD = 128
@@ -29,6 +31,177 @@
     units = (jax.nn.silu(gate_act) * up_act).astype(jnp.bfloat16)
     part = jnp.dot(units, expert_down[0], preferred_element_type=jnp.float32)
     return (part * gate).astype(jnp.bfloat16)
+
+
+def scatter_kernel(
+    in_ref, out_ref, core_in, acc, diag_x, diag_y, from_x, from_y, z_send, z_up, z_down, sends, recvs
+):
+    x = lax.axis_index("dp")
+    e = lax.axis_index("expert")
+    z, y, c = e // 4, (e // 2) % 2, e % 2
+    half = in_ref.shape[4] // 2
+    high = z // 2
+    low_z = z + high * (3 - 2 * z)
+    order = [f + high * (3 - 2 * f) for f in (3 + 0 * z, 2 - 2 * low_z, 1 + low_z, low_z)]
+    other_core = {"expert": e + 1 - 2 * c}
+    other_y = {"expert": e + 2 - 4 * y}
+    other_x = {"dp": 1 - x}
+    above, below = {"expert": e + 4}, {"expert": e - 4}
+
+    def copy(src, dst, kind, k, to):
+        return pltpu.make_async_remote_copy(
+            src_ref=src,
+            dst_ref=dst,
+            send_sem=sends.at[kind, k],
+            recv_sem=recvs.at[kind, k],
+            device_id=to,
+            device_id_type=pl.DeviceIdType.MESH,
+        )
+
+    def core_copy(k):
+        return copy(in_ref.at[order[k], :, 1 - c], core_in.at[k], 0, k, other_core)
+
+    def diag_y_copy(k):
+        return copy(acc.at[k, 1 - y, 1 - x, pl.ds(0, half)], diag_y.at[k], 1, k, other_y)
+
+    def diag_x_copy(k):
+        return copy(acc.at[k, 1 - y, 1 - x, pl.ds(half, half)], diag_x.at[k], 2, k, other_x)
+
+    def x_copy(k):
+        return copy(acc.at[k, y, 1 - x], from_x.at[k], 3, k, other_x)
+
+    def y_copy(k):
+        return copy(acc.at[k, 1 - y, x], from_y.at[k], 4, k, other_y)
+
+    def up_copy(k):
+        return copy(z_send.at[order[k]], z_up.at[order[k]], 5, order[k], above)
+
+    def down_copy(k):
+        return copy(z_send.at[order[k]], z_down.at[order[k]], 6, order[k], below)
+
+    def wide(value):
+        return value.astype(jnp.float32)
+
+    barrier = pltpu.get_barrier_semaphore()
+    for to in (other_core, other_x, other_y):
+        pl.semaphore_signal(barrier, inc=1, device_id=to, device_id_type=pl.DeviceIdType.MESH)
+
+    @pl.when(z > 0)
+    def _():
+        pl.semaphore_signal(barrier, inc=1, device_id=below, device_id_type=pl.DeviceIdType.MESH)
+
+    @pl.when(z < 3)
+    def _():
+        pl.semaphore_signal(barrier, inc=1, device_id=above, device_id_type=pl.DeviceIdType.MESH)
+
+    pl.semaphore_wait(barrier, 4 + ((z + 1) // 2) % 2)
+
+    for k in range(4):
+        core_copy(k).start()
+
+    def stage_a(k):
+        core_copy(k).wait_recv()
+        for j in (0, 1):
+            for i in (0, 1):
+                acc[k, j, i] = (wide(in_ref[order[k], j, c, i]) + wide(core_in[k, j, i])).astype(
+                    acc.dtype
+                )
+        diag_y_copy(k).start()
+        diag_x_copy(k).start()
+
+    def stage_b(k):
+        top, bottom = pl.ds(0, half), pl.ds(half, half)
+        diag_y_copy(k).wait_recv()
+        acc[k, y, 1 - x, top] = (wide(acc[k, y, 1 - x, top]) + wide(diag_y[k])).astype(acc.dtype)
+        x_copy(k).start()
+        diag_x_copy(k).wait_recv()
+        acc[k, 1 - y, x, bottom] = (wide(acc[k, 1 - y, x, bottom]) + wide(diag_x[k])).astype(
+            acc.dtype
+        )
+        y_copy(k).start()
+
+    def stage_c(k):
+        x_copy(k).wait_recv()
+        y_copy(k).wait_recv()
+        g = order[k]
+        out_ref[...] = wide(acc[k, y, x]) + wide(from_x[k]) + wide(from_y[k])
+
+        @pl.when((g >= z) & (z > 0))
+        def _():
+            up_copy(k).wait_recv()
+            out_ref[...] += wide(z_up[g])
+
+        @pl.when((g <= z) & (z < 3))
+        def _():
+            down_copy(k).wait_recv()
+            out_ref[...] += wide(z_down[g])
+
+        if k < 3:
+            z_send[g] = out_ref[...].astype(z_send.dtype)
+
+            @pl.when(g > z)
+            def _():
+                up_copy(k).start()
+
+            @pl.when(g < z)
+            def _():
+                down_copy(k).start()
+
+    stage_a(0)
+    stage_a(1)
+    stage_b(0)
+    stage_a(2)
+    stage_b(1)
+    stage_c(0)
+    stage_a(3)
+    stage_b(2)
+    stage_c(1)
+    stage_b(3)
+    stage_c(2)
+    stage_c(3)
+    for k in range(4):
+        for made in (core_copy, diag_y_copy, diag_x_copy, x_copy, y_copy):
+            made(k).wait_send()
+        if k < 3:
+
+            @pl.when(order[k] > z)
+            def _():
+                up_copy(k).wait_send()
+
+            @pl.when(order[k] < z)
+            def _():
+                down_copy(k).wait_send()
+
+
+def scatter_sum(part):
+    if lax.axis_size("dp") != 2 or lax.axis_size("expert") != 16:
+        return lax.psum_scatter(
+            part, ("expert", "dp"), scatter_dimension=0, tiled=True
+        ).astype(jnp.float32)
+    rows, width = part.shape[0] // 32, part.shape[1]
+    kind = part.dtype
+    return pl.pallas_call(
+        scatter_kernel,
+        out_shape=jax.ShapeDtypeStruct((rows, width), jnp.float32),
+        in_specs=[pl.BlockSpec(memory_space=pltpu.VMEM)],
+        out_specs=pl.BlockSpec(memory_space=pltpu.VMEM),
+        scratch_shapes=[
+            pltpu.VMEM((4, 2, 2, rows, width), kind),
+            pltpu.VMEM((4, 2, 2, rows, width), kind),
+            pltpu.VMEM((4, rows // 2, width), kind),
+            pltpu.VMEM((4, rows // 2, width), kind),
+            pltpu.VMEM((4, rows, width), kind),
+            pltpu.VMEM((4, rows, width), kind),
+            pltpu.VMEM((4, rows, width), kind),
+            pltpu.VMEM((4, rows, width), kind),
+            pltpu.VMEM((4, rows, width), kind),
+            pltpu.SemaphoreType.DMA((7, 4)),
+            pltpu.SemaphoreType.DMA((7, 4)),
+        ],
+        compiler_params=pltpu.CompilerParams(
+            collective_id=0, has_side_effects=True, vmem_limit_bytes=48 * 2**20
+        ),
+    )(part.reshape(4, 2, 2, 2, rows, width))
 
 
 def per_device(
@@ -109,24 +282,33 @@
         lax.dynamic_slice_in_dim(residual[0], start, block_rows, 0).astype(jnp.float32) + attended
     )
     normed = norm_rows(hidden_mine, norm_gain)
-    everyone = lax.all_gather(normed, ("expert", "dp"), axis=0, tiled=True)
+    ids_mine = lax.dynamic_slice_in_dim(expert_ids[0], start, block_rows, 0)
+    weights_mine = lax.dynamic_slice_in_dim(expert_weights[0], start, block_rows, 0)
     gates = jnp.sum(
         jnp.where(
-            expert_ids[0][:, :, None] == jnp.arange(experts_all)[None, None, :],
-            expert_weights[0][:, :, None],
+            ids_mine[:, :, None] == jnp.arange(experts_all)[None, None, :],
+            weights_mine[:, :, None],
             0.0,
         ),
         axis=1,
     )
-    all_gates = lax.all_gather(gates, "expert", axis=0, tiled=True)
+    gates_high = gates.astype(jnp.bfloat16)
+    gates_low = (gates - gates_high.astype(jnp.float32)).astype(jnp.bfloat16)
+    model = normed.shape[1]
+    extra = -(-2 * experts_all // 128) * 128
+    fill = jnp.zeros((block_rows, extra - 2 * experts_all), jnp.bfloat16)
+    sent = jnp.concatenate([normed, gates_high, gates_low, fill], axis=1)
+    gathered = lax.all_gather(sent, ("expert", "dp"), axis=0, tiled=True)
+    everyone = gathered[:, :model]
     mine = lax.axis_index("expert")
+    named = (jnp.arange(extra) == mine) | (jnp.arange(extra) == mine + experts_all)
     gate = jnp.sum(
-        jnp.where(jnp.arange(experts_all)[None, :] == mine, all_gates, 0.0), axis=1, keepdims=True
+        jnp.where(named[None, :], gathered[:, model:].astype(jnp.float32), 0.0),
+        axis=1,
+        keepdims=True,
     )
     part = expert_apply(everyone, gate, expert_in, expert_down)
-    mixture = lax.psum_scatter(
-        part, ("expert", "dp"), scatter_dimension=0, tiled=True
-    ).astype(jnp.float32)
+    mixture = scatter_sum(part)
     layer_out = (hidden_mine + mixture).astype(jnp.bfloat16)[None]
     return (layer_out, mixture.astype(jnp.bfloat16)[None])
 

time: 368 us -> 234 us (0.64)
  waiting for transfers between devices: 248 us -> 84.1 us
  Pallas kernels: 0 us -> 43.7 us
  blocking collectives: 27 us -> 10.7 us
    reduce_scatter x1 -> x0, waiting for transfers between devices: 181 us -> none  [per_device(): lax.psum_scatter(part, ('expert', 'dp'), scatter_dimension=0, tiled=True)]
    pallas_call x0 -> x1, Pallas kernels: none -> 43.7 us  [scatter_sum(): pl.pallas_call(scatter_kernel, out_shape=jax.ShapeDtypeStruct((rows, widt...]
    all_gather x1, waiting for transfers between devices: 49 us -> 67 us  [per_device(): gathered = lax.all_gather(sent, ('expert', 'dp'), axis=0, tiled=True)]
    all_gather x1 -> x0, blocking collectives: 16.3 us -> none  [per_device(): all_gates = lax.all_gather(gates, 'expert', axis=0, tiled=True)]
  transfers between devices with their start and end apart: 3 -> 2, of which waited for: 3 -> 2; matrix products, arithmetic and copies ran while one was open for 4% -> 6% of each run, Pallas kernels for 0% -> 0%
where the time goes in v2:
time: 234 us; the launch traced here: 231 us
  waiting for transfers between devices  84.1 us (36%)
  matrix products  50.4 us (22%)
  Pallas kernels  43.7 us (19%)
  local copies, waits for them, and re-layouts  20.1 us (9%)
  between operations  15 us (6%)
  blocking collectives  10.7 us (5%)
  other arithmetic  7 us (3%)
    all_gather x1, waiting for transfers between devices, per_device(): gathered = lax.all_gather(sent, ('expert', 'dp'), axis=0, tiled=True)  67 us
    pallas_call x1, Pallas kernels, scatter_sum(): pl.pallas_call(scatter_kernel, out_shape=jax.ShapeDtypeStruct((rows, widt...  43.7 us
    dot_general x1, matrix products, expert_apply(): part = jnp.dot(units, expert_down[0], preferred_element_type=jnp.float32)  20.9 us
    reduce_scatter x1, waiting for transfers between devices, per_device(): lax.psum_scatter(partial_out.astype(jnp.bfloat16), 'dp', scatter_dimensio...  17.1 us
    dot_general x1, matrix products, expert_apply(): lax.dot_general(flat, expert_in[0, :, 0, :], dims, preferred_element_type...  13 us
    slice x1, local copies, waits for them, and re-layouts, expert_apply(): expert_in[0, :, 1, :]  12.8 us
    all_gather x1, blocking collectives, per_device(): lax.all_gather(latent_pages[0], 'dp', axis=0, tiled=True)  6.9 us
    sub x1, matrix products, per_device(): expo = jnp.where(allowed, jnp.exp(masked - peak), 0.0)  4.9 us
  transfers between devices with their start and end apart: 2, of which 2 were waited for; matrix products, arithmetic and copies ran while one was open for 6% of the time, Pallas kernels for 0%

profile of v2, /device:TPU:13, one launch (start us, length us, event | category | flops | bytes accessed | tf_op | source)
XLA Modules:
  0.0 231.3 jit_solution(1228627435822497195)
XLA Ops:
  8.1 0.8 select_reduce_fusion.2
  8.8 0.1 add_compare_fusion
  8.9 0.1 reshape.80
  9.0 0.8 copy.66
  9.8 3.8 %all-gather.1 = bf16[1,8,4096]{2,0,1:T(2,128)(2,1)S(1)} all-gather(bf16[1,4,4096]{2,0,1:T(2,128)(2,1)S(1)} %copy.66), channel_id=3, replica_groups=mesh['dp'=2,'expert'=16] {'dp'}, dimensions={1}, use_global_device_ids=true | all-gather | bytes 98304 | tf_op jit(solution)/shard_map/all_gather | solution.py:233
  13.6 0.4 reduce
  14.0 0.2 reshape.69
  14.1 0.7 copy.67
  14.9 1.7 copy.68
  16.5 1.7 copy.86
  18.2 6.9 %all-gather = bf16[1,8,64,512]{3,2,0,1:T(8,128)(2,1)S(1)} all-gather(bf16[1,4,64,512]{3,2,0,1:T(8,128)(2,1)} %bitcast.72), channel_id=2, replica_groups=mesh['dp'=2,'expert'=16] {'dp'}, dimensions={1}, use_global_device_ids=true | all-gather | bytes 786432 | tf_op jit(solution)/shard_map/all_gather | solution.py:232
  25.1 0.7 pad_add_fusion
  25.8 4.1 %fusion.14 = f32[128,8,640]{2,0,1:T(8,128)} fusion(bf16[8,128,512]{2,1,0:T(8,128)(2,1)} %param.26, bf16[128,512]{1,0:T(8,128)(2,1)} %bitcast.75, bf16[512,512]{1,0:T(8,128)(2,1)S(1)} %bitcast.69, bf16[128,8,128]{2,1,0:T(8,128)(2,1)} %bitcast.71), kind=kOutput, calls=%fused_computation.19 | convolution fusion | flops 807141376 | bytes 4587520 | tf_op jit(solution)/shard_map/thc,kc->thk/dot_general | solution.py:254
  29.9 4.9 %fusion.34 = (f32[128,8]{0,1:T(8,128)}, bf16[128,8,640]{2,0,1:T(8,128)(2,1)}) fusion(pred[128,640]{1,0:T(8,128)(4,1)} %pad_add_fusion, f32[128,8,640]{2,0,1:T(8,128)} %fusion.14, bf16[128,8,64]{0,2,1:T(8,128)(2,1)} %bitcast.77, bf16[128,64]{0,1:T(8,128)(2,1)S(1)} %bitcast.80, bf16[512,64]{0,1:T(8,128)(2,1)} %copy.67), kind=kOutput, calls=%fused_computation.56 | convolution fusion | flops 88638080 | bytes 4231168 | tf_op jit(solution)/shard_map/sub | solution.py:263
  34.8 3.6 %fusion.19 = bf16[8,128,128]{1,2,0:T(8,128)(2,1)} fusion(bf16[8,512,128]{2,1,0:T(8,128)(2,1)} %param.27, bf16[128,8,640]{2,0,1:T(8,128)(2,1)} %get-tuple-element.7, f32[128,8]{0,1:T(8,128)} %get-tuple-element.6, bf16[128,512]{1,0:T(8,128)(2,1)S(1)} %bitcast.76, bf16[512,512]{1,0:T(8,128)(2,1)S(1)} %bitcast.70), kind=kOutput, calls=%fused_computation.22 | convolution fusion | flops 807796736 | bytes 3280896 | tf_op jit(solution)/shard_map/thc,hcd->thd/dot_general | solution.py:269
  38.4 3.9 %convolution_convert_fusion = bf16[128,2048]{1,0:T(8,128)(2,1)} fusion(bf16[128,1024]{0,1:T(8,128)(2,1)} %bitcast.73, bf16[1024,2048]{1,0:T(8,128)(2,1)} %param.28), kind=kOutput, calls=%fused_computation.15 | convolution fusion | flops 537133056 | bytes 4980736 | tf_op jit(solution)/shard_map/dot_general | solution.py:272
  42.3 0.2 all-gather.4.cloned.1.call-start
  42.6 0.1 constant_dynamic-slice_fusion.1
  42.7 0.1 constant_dynamic-slice_fusion
  42.8 0.1 copy.74
  42.9 0.1 copy.75
  43.0 17.1 %reduce-scatter.2.cloned.1.call-done = bf16[64,2048]{1,0:T(8,128)(2,1)} async-done(((bf16[128,2048]{1,0:T(8,128)(2,1)}), bf16[64,2048]{1,0:T(8,128)(2,1)}) %reduce-scatter.2.cloned.1.call-update) | async-done | bytes 262160 | tf_op jit(solution)/shard_map/reduce_scatter | solution.py:277
  60.1 1.1 multiply_reduce_fusion
  61.2 1.8 multiply_convert_fusion.2
  63.0 1.7 concatenate.15
  64.8 12.8 %fusion.33 = (bf16[1,704,1,2048]{3,2,1,0:T(2,128)(2,1)}, bf16[1,704,1,2048]{3,2,1,0:T(2,128)(2,1)}) fusion(bf16[1,704,2,2048]{3,2,1,0:T(2,128)(2,1)} %param.30), kind=kLoop, calls=%fused_computation.55 | loop fusion | bytes 11534336 | tf_op jit(solution)/shard_map/slice | solution.py:30
  77.6 67.0 %all-gather.4.cloned.1.call-done = bf16[2048,2176]{1,0:T(8,128)(2,1)} async-done(((bf16[64,2176]{1,0:T(8,128)(2,1)}), bf16[2048,2176]{1,0:T(8,128)(2,1)}) %all-gather.4.cloned.1.call-update) | async-done | bytes 8912912 | tf_op jit(solution)/shard_map/all_gather | solution.py:301
  144.6 1.3 select_reduce_fusion
  145.9 13.0 %fusion.3 = f32[2048,704]{0,1:T(8,128)} fusion(bf16[2048,2176]{1,0:T(8,128)(2,1)} %all-gather.4.cloned.1.call-done, bf16[1,704,1,2048]{3,2,1,0:T(2,128)(2,1)} %get-tuple-element.3), kind=kOutput, calls=%fused_computation.4 | convolution fusion | flops 5905580032 | bytes 19922944 | tf_op jit(solution)/shard_map/dot_general | solution.py:27
  158.9 20.9 %multiply_convert_fusion = bf16[2048,2048]{1,0:T(8,128)(2,1)} fusion(f32[2048]{0:T(1024)S(1)} %select_reduce_fusion, f32[2048,704]{0,1:T(8,128)} %fusion.3, bf16[2048,2176]{1,0:T(8,128)(2,1)} %all-gather.4.cloned.1.call-done, bf16[1,704,1,2048]{3,2,1,0:T(2,128)(2,1)} %get-tuple-element.2, bf16[1,704,2048]{2,1,0:T(8,128)(2,1)S(1)} %copy-done), kind=kOutput, calls=%fused_computation.1 | convolution fusion | flops 11828199424 | bytes 31203328 | tf_op jit(solution)/shard_map/dot_general | solution.py:32
  179.8 43.7 %shard_map.176 = f32[64,2048]{1,0:T(8,128)S(1)} custom-call(bf16[4,2,2,2,64,2048]{5,4,3,2,1,0:T(8,128)(2,1)} %bitcast.68), custom_call_target="tpu_custom_call" | custom-call | tf_op jit(solution)/shard_map/pallas_call | solution.py:183
  223.5 0.9 convert_bitcast_fusion
  (30 shorter events, 0.2 us)
Async XLA Ops:
  7.2 151.7 %copy-start = (bf16[1,704,2048]{2,1,0:T(8,128)(2,1)S(1)}, bf16[1,704,2048]{2,1,0:T(8,128)(2,1)}, u32[]{:S(2)}) copy-start(bf16[1,704,2048]{2,1,0:T(8,128)(2,1)} %param.31) | copy-start | bytes 8650756
  7.2 22.7 %copy-start.7 = (bf16[1,128,64]{1,2,0:T(8,128)(2,1)S(1)}, bf16[1,128,64]{1,2,0:T(8,128)(2,1)}, u32[]{:S(2)}) copy-start(bf16[1,128,64]{1,2,0:T(8,128)(2,1)} %param.20) | copy-start | bytes 49156
  7.2 52.9 %reduce-scatter.2.cloned.1.call-start = ((), (), s32[]{:S(2)}) async-start(), calls=%async_computation.1 | async-start | bytes 786432 | tf_op jit(solution)/shard_map/reduce_scatter | solution.py:277
  29.9 4.9 %copy-start.3 = (bf16[1,128,512]{2,1,0:T(8,128)(2,1)S(1)}, bf16[1,128,512]{2,1,0:T(8,128)(2,1)}, u32[]{:S(2)}) copy-start(bf16[1,128,512]{2,1,0:T(8,128)(2,1)} %param.19) | copy-start | bytes 393220
  38.4 4.1 %copy-start.5 = (s32[1,128,6]{1,0,2:T(1,128)S(1)}, s32[1,128,6]{1,0,2:T(1,128)}, u32[]{:S(2)}) copy-start(s32[1,128,6]{1,0,2:T(1,128)} %param.32) | copy-start | bytes 9220
  38.4 4.2 %copy-start.6 = (f32[1,128,6]{1,0,2:T(1,128)S(1)}, f32[1,128,6]{1,0,2:T(1,128)}, u32[]{:S(2)}) copy-start(f32[1,128,6]{1,0,2:T(1,128)} %param.33) | copy-start | bytes 9220
  38.4 21.6 %copy-start.2 = (bf16[1,128,2048]{2,1,0:T(8,128)(2,1)S(1)}, bf16[1,128,2048]{2,1,0:T(8,128)(2,1)}, u32[]{:S(2)}) copy-start(bf16[1,128,2048]{2,1,0:T(8,128)(2,1)} %param.25) | copy-start | bytes 1572868
  38.4 22.8 %copy-start.4 = (f32[2048]{0:T(1024)S(1)}, f32[2048]{0:T(1024)}, u32[]{:S(2)}) copy-start(f32[2048]{0:T(1024)} %param.29) | copy-start | bytes 24580
  42.3 102.3 %all-gather.4.cloned.1.call-start = ((), (), s32[]{:S(2)}) async-start(), calls=%async_computation.2 | async-start | bytes 9191424 | tf_op jit(solution)/shard_map/all_gather | solution.py:301
  179.8 43.7 %copy-start.1 = (bf16[64,2048]{1,0:T(8,128)(2,1)S(1)}, bf16[64,2048]{1,0:T(8,128)(2,1)}, u32[]{:S(2)}) copy-start(bf16[64,2048]{1,0:T(8,128)(2,1)} %reduce-scatter.2.cloned.1.call-done) | copy-start | bytes 786436
Sparse Core Ops, SparseCore 0:
  42.5 17.5 reduce-scatter.1
  64.9 79.6 all-gather.3
